TPU v7x, 256 devices: a whole 4x4x8 slice. The times are simulated.
256 devices in a mesh: col: 32 (over z, x), row: 8 (over y, core).
Axes of the slice: x: 4, y: 4, z: 8, core: 2. Of those that a mesh axis runs over, the one named last changes fastest.
Arguments:
- trailing: float32 [24576, 16384], P('row', 'col'), may hold values from -6 to 6
- panel_rows: float32 [24576, 512], P(('row', 'col')), may hold values from -6 to 6
- pivot_block: float32 [512, 512], P('col'), as said below
- panel_fill: int32 [96, 2], replicated, may hold values 0 or 1
Outputs:
- updated: float32 [24576, 16384], P('row', 'col')
- panel_factor: float32 [24576, 512], P(('row', 'col'))
Inputs may be any that keep to these rules, and one draw needn't show every extreme that they name: `pivot_block`: Symmetric; each diagonal entry exceeds the sum of the magnitudes of the other entries of its row by at least 1. `panel_fill`: each entry is 1 with probability 0.15, independently of the others.
All inputs are finite; a program needn't handle non-finite values.
Results may differ from a plain program's by a relative error of at most 0.00008.
Values sent between devices are 32-bit elements; how exact they have to be, the bound alone decides.
A program may use at most 128 MiB of HBM per device.

v0:
```python
import jax
import jax.numpy as jnp
from jax import lax
from jax.sharding import PartitionSpec as P


def from_root(value, axis, source):
    kept = jnp.where(lax.axis_index(axis) == source, value, 0).astype(value.dtype)
    return lax.psum(kept, axis)


def apply_fill(values, row_start, fill_table, block_size):
    row_count = values.shape[0]
    blocks = (row_start + jnp.arange(row_count, dtype=jnp.int32)) // block_size
    one_hot = (blocks[:, None] == jnp.arange(fill_table.shape[0], dtype=jnp.int32)[None, :]).astype(
        jnp.float32
    )
    flags = jnp.dot(one_hot, fill_table.astype(jnp.float32), precision=lax.Precision.HIGHEST)
    shaped = values.reshape(row_count, 2, block_size) * flags[:, :, None]
    return shaped.reshape(row_count, 2 * block_size)


def solve_rows(values, factor):
    return lax.linalg.triangular_solve(
        factor, values, left_side=False, lower=True, transpose_a=True
    )


def per_device(trailing, panel_rows, pivot_block, panel_fill):
    block_size = panel_rows.shape[1] // 2
    piece_rows = panel_rows.shape[0]
    col_count = lax.axis_size("col")
    col_index = lax.axis_index("col")
    row_index = lax.axis_index("row")
    local_rows = piece_rows * col_count
    slab_start = row_index * local_rows
    pivot_full = lax.all_gather(pivot_block, "col", axis=0, tiled=True)
    factor = jnp.linalg.cholesky(pivot_full)
    piece_start = slab_start + col_index * piece_rows
    own_factor = solve_rows(apply_fill(panel_rows, piece_start, panel_fill, block_size), factor)
    row_side = lax.all_gather(own_factor, "col", axis=0, tiled=True)
    column_count = trailing.shape[1]
    column_start = col_index * column_count
    owner_row = column_start // local_rows
    offered = lax.dynamic_slice_in_dim(row_side, column_start - slab_start, column_count, 0)
    column_side = from_root(offered, "row", owner_row)
    update = lax.dot_general(
        row_side,
        column_side,
        (((1,), (1,)), ((), ())),
        precision=lax.Precision.HIGHEST,
        preferred_element_type=jnp.float32,
    )
    return (trailing - update, own_factor)


def solution(mesh):
    in_specs = (P("row", "col"), P(("row", "col"), None), P("col", None), P())
    out_specs = (P("row", "col"), P(("row", "col"), None))
    return jax.shard_map(
        per_device, mesh=mesh, in_specs=in_specs, out_specs=out_specs, check_vma=False
    )
```

profile of v0, /device:TPU:6, one launch (start us, length us, event | category | flops | bytes accessed | tf_op | source)
XLA Modules:
  0.0 402.1 jit_solution(7585898141999107908)
XLA Ops:
  7.2 0.7 all-gather.3.cloned.1.call-update
  8.0 0.9 fusion.28
  9.1 1.0 mul.24
  10.0 78.7 %all-gather.3.cloned.1.call-done = f32[512,512]{1,0:T(8,128)} async-done(((f32[16,512]{1,0:T(8,128)}), f32[512,512]{1,0:T(8,128)}) %all-gather.3.cloned.1.call-update) | async-done | bytes 1048592 | tf_op jit(solution)/shard_map/all_gather | solution.py:37
  88.7 1.6 copy.10
  90.3 1.4 fusion
  91.7 11.7 %cholesky.104 = f32[128,128]{1,0:T(8,128)S(1)} custom-call(f32[128,128]{1,0:T(8,128)S(1)} %cholesky.266), custom_call_target="Cholesky" | custom-call | tf_op jit(solution)/shard_map/jit(cholesky)/cholesky | solution.py:38
  103.5 9.8 %custom-call.30 = f32[1,128,128]{1,2,0:T(8,128)S(1)} custom-call(f32[1,128,128]{2,1,0:T(8,128)S(1)} %get-tuple-element.29), custom_call_target="InvertDiagBlocksLowerTriangular" | custom-call | tf_op jit(solution)/shard_map/jit(cholesky)/cholesky | solution.py:38
  114.1 11.7 %cholesky.217 = f32[128,128]{1,0:T(8,128)S(1)} custom-call(f32[128,128]{1,0:T(8,128)S(1)} %cholesky.270), custom_call_target="Cholesky" | custom-call | tf_op jit(solution)/shard_map/jit(cholesky)/cholesky | solution.py:38
  125.9 10.0 %custom-call.31 = f32[1,128,128]{1,2,0:T(8,128)S(1)} custom-call(f32[1,128,128]{2,1,0:T(8,128)S(1)} %get-tuple-element.26), custom_call_target="InvertDiagBlocksLowerTriangular" | custom-call | tf_op jit(solution)/shard_map/jit(cholesky)/cholesky | solution.py:38
  136.5 11.7 %cholesky.238 = f32[128,128]{1,0:T(8,128)S(1)} custom-call(f32[128,128]{1,0:T(8,128)S(1)} %cholesky.275), custom_call_target="Cholesky" | custom-call | tf_op jit(solution)/shard_map/jit(cholesky)/cholesky | solution.py:38
  148.2 0.7 compare_reduce_fusion.1
  149.0 9.8 %custom-call.32 = f32[1,128,128]{1,2,0:T(8,128)S(1)} custom-call(f32[1,128,128]{2,1,0:T(8,128)S(1)} %get-tuple-element.23), custom_call_target="InvertDiagBlocksLowerTriangular" | custom-call | tf_op jit(solution)/shard_map/jit(cholesky)/cholesky | solution.py:38
  159.4 11.9 %cholesky.255 = f32[128,128]{1,0:T(8,128)S(1)} custom-call(f32[128,128]{1,0:T(8,128)S(1)} %convolution_subtract_fusion.3), custom_call_target="Cholesky" | custom-call | tf_op jit(solution)/shard_map/jit(cholesky)/cholesky | solution.py:38
  171.3 0.6 compare_reduce_fusion
  171.9 0.7 compare_reduce_fusion.2
  175.3 8.5 %while.1 = (s32[]{:T(128)}, f32[512,512]{1,0:T(8,128)S(1)}, s32[4,2]{0,1:T(2,128)S(1)}, f32[4,128,128]{2,1,0:T(8,128)S(1)}, s32[]{:T(128)}) while((s32[]{:T(128)}, f32[512,512]{1,0:T(8,128)S(1)}, s32[4,2]{0,1:T(2,128)S(1)}, f32[4,128,128]{2,1,0:T(8,128)S(1)}, s32[]{:T(128)}) %tuple.31), condition=%wide.while_cond, body=%wide.while_body.sunk | while | flops 2 | bytes 131189 | solution.py:24
  175.3 0.6 fusion.42
  175.9 1.4 bitcast_dynamic-update-slice_fusion.2
  177.5 0.6 fusion.42
  178.1 1.4 bitcast_dynamic-update-slice_fusion.2
  179.6 0.6 fusion.42
  180.2 1.4 bitcast_dynamic-update-slice_fusion.2
  181.7 0.6 fusion.42
  182.3 1.4 bitcast_dynamic-update-slice_fusion.2
  183.7 39.3 %custom-call.33 = f32[4,128,128]{1,2,0:T(8,128)S(1)} custom-call(f32[4,128,128]{2,1,0:T(8,128)S(1)} %get-tuple-element.9), custom_call_target="InvertDiagBlocksLowerTriangular" | custom-call | tf_op jit(solution)/shard_map/triangular_solve | solution.py:24
  224.2 0.4 convolution_subtract_fusion.6
  224.8 0.7 pad_maximum_fusion
  225.6 85.5 %all-gather.5.cloned.1.call-done = f32[3072,512]{1,0:T(8,128)} async-done(((f32[96,512]{1,0:T(8,128)}), f32[3072,512]{1,0:T(8,128)}) %all-gather.5.cloned.1.call-update) | async-done | bytes 6291472 | tf_op jit(solution)/shard_map/all_gather | solution.py:41
  311.1 2.3 dynamic-slice_select_fusion
  313.4 67.1 %all-reduce.3.cloned.1.call-done = f32[512,512]{1,0:T(8,128)} async-done(((f32[512,512]{1,0:T(8,128)}), f32[512,512]{1,0:T(8,128)}) %all-reduce.3.cloned.1.call-update) | async-done | bytes 1048592 | tf_op jit(solution)/shard_map/psum | solution.py:9
  380.5 15.1 %convolution_subtract_fusion = f32[3072,512]{1,0:T(8,128)} fusion(f32[3072,512]{1,0:T(8,128)} %param.4, f32[3072,512]{1,0:T(8,128)} %all-gather.5.cloned.1.call-done, f32[512,512]{1,0:T(8,128)} %all-reduce.3.cloned.1.call-done), kind=kOutput, calls=%fused_computation.2 | convolution fusion | flops 9665249280 | bytes 19922944 | tf_op jit(solution)/shard_map/dot_general | solution.py:47
  (36 shorter events, 4.2 us)
Async XLA Ops:
  7.2 81.6 %all-gather.3.cloned.1.call-start = ((), (), s32[]{:S(2)}) async-start(), calls=%async_computation | async-start | bytes 1081344 | tf_op jit(solution)/shard_map/all_gather | solution.py:37
  7.9 303.2 %all-gather.5.cloned.1.call-start = ((), (), s32[]{:S(2)}) async-start(), calls=%async_computation.1 | async-start | bytes 6488064 | tf_op jit(solution)/shard_map/all_gather | solution.py:41
  225.5 155.0 %all-reduce.3.cloned.1.call-start = ((), (), s32[]{:S(2)}) async-start(), calls=%async_computation.2 | async-start | bytes 2097152 | tf_op jit(solution)/shard_map/psum | solution.py:9
Sparse Core Ops, SparseCore 0:
  10.6 78.0 all-gather.2
  225.6 85.4 all-gather.4
  314.1 66.3 all-reduce.2
where the time goes:
time: 403 us; the launch traced here: 402 us
  waiting for transfers between devices  232 us (58%)
  other arithmetic  124 us (31%)
  matrix products  19.6 us (5%)
  between operations  16.6 us (4%)
  local copies, waits for them, and re-layouts  10.3 us (3%)
    all_gather x1, waiting for transfers between devices, per_device(): row_side = lax.all_gather(own_factor, 'col', axis=0, tiled=True)  85.5 us
    another operation x14, other arithmetic, per_device(): factor = jnp.linalg.cholesky(pivot_full)  78.7 us
    all_gather x1, waiting for transfers between devices, per_device(): pivot_full = lax.all_gather(pivot_block, 'col', axis=0, tiled=True)  78.7 us
    psum x1, waiting for transfers between devices, from_root(): return lax.psum(kept, axis)  67.1 us
    another operation x4, other arithmetic, solve_rows(): lax.linalg.triangular_solve(factor, values, left_side=False, lower=True,...  40.1 us
    dot_general x1, matrix products, per_device(): lax.dot_general(row_side, column_side, (((1,), (1,)), ((), ())), precisio...  15.1 us
    another operation x12, local copies, waits for them, and re-layouts  8.39 us
  transfers between devices with their start and end apart: 3, of which 3 were waited for; matrix products, arithmetic and copies ran while one was open for 1% of the time, Pallas kernels for 0%

commit v1 on v0

v1 whole, which is shorter than its diff:
```python
import functools

import jax
import jax.numpy as jnp
from jax import lax
from jax.experimental import pallas as pl
from jax.experimental.pallas import tpu as pltpu
from jax.sharding import PartitionSpec as P

F32 = jnp.float32
BF16 = jnp.bfloat16
HIGHEST = lax.Precision.HIGHEST
NT = (((1,), (1,)), ((), ()))
NN = (((1,), (0,)), ((), ()))
TN = (((0,), (0,)), ((), ()))

ZS, XS = 8, 4
COLS, ROWS = ZS * XS, 8
B = 256
TILE = 128


def mm(a, b, dims):
    return lax.dot_general(a, b, dims, precision=HIGHEST, preferred_element_type=F32)


def split(v):
    hi = v.astype(BF16)
    return hi, (v - hi.astype(F32)).astype(BF16)


def mm3(a, b, dims):
    dot = functools.partial(lax.dot_general, dimension_numbers=dims, preferred_element_type=F32)
    return dot(a[0], b[0]) + (dot(a[0], b[1]) + dot(a[1], b[0]))


def spread_row(v, r):
    return jnp.broadcast_to(v[r : r + 1, :], v.shape)


def invert_tile(groups, hook):
    n = groups[0].shape[1]
    count = n // 8
    lane = lax.broadcasted_iota(jnp.int32, (8, n), 1)
    sub = lax.broadcasted_iota(jnp.int32, (8, n), 0)
    left = list(groups)
    right = [jnp.where(lane == sub + 8 * g, 1.0, 0.0).astype(F32) for g in range(count)]
    done = []

    def columns(h, g):
        return [
            jnp.broadcast_to(left[h][:, 8 * g + r : 8 * g + r + 1], (8, n)) for r in range(8)
        ]

    def total(terms):
        while len(terms) > 1:
            terms = [a + b for a, b in zip(terms[::2], terms[1::2])]
        return terms[0]

    for g in range(count):
        hook(g)
        pivot = columns(g, g)
        below = {h: columns(h, g) for h in range(g + 1, count)}
        wide, inv = left[g], right[g]
        final = inv
        for r in range(0, 8, 2):
            a, b, d = (
                spread_row(pivot[r], r),
                spread_row(pivot[r + 1], r),
                spread_row(pivot[r + 1], r + 1),
            )
            det = a * d - b * b
            scale = 1.0 / det
            an, bn, dn = a * scale, b * scale, d * scale
            m0, m1 = pivot[r], pivot[r + 1]
            e0, e1 = spread_row(inv, r), spread_row(inv, r + 1)
            over_a = 1.0 / a
            f0 = e0 * lax.rsqrt(a)
            f1 = (e1 - (b * over_a) * e0) * lax.rsqrt(det * over_a)
            final = jnp.where(sub == r, f0, jnp.where(sub == r + 1, f1, final))

            def step(w):
                w0, w1 = spread_row(w, r), spread_row(w, r + 1)
                y0 = dn * w0 - bn * w1
                y1 = an * w1 - bn * w0
                rest = w - (m0 * y0 + m1 * y1)
                return jnp.where(sub == r, y0, jnp.where(sub == r + 1, y1, rest))

            for q in range(r + 2, 8):
                pivot[q] = step(pivot[q])
            wide, inv = step(wide), step(inv)
        done.append(final)
        wide_rows = [spread_row(wide, r) for r in range(8)]
        inv_rows = [spread_row(inv, r) for r in range(8)]
        for h in range(g + 1, count):
            left[h] = left[h] - total([below[h][r] * wide_rows[r] for r in range(8)])
            right[h] = right[h] - total([below[h][r] * inv_rows[r] for r in range(8)])
    return done

SLOTS = 8


def remote(src, dst, send, recv, col, row):
    return pltpu.make_async_remote_copy(
        src_ref=src, dst_ref=dst, send_sem=send, recv_sem=recv,
        device_id={"col": col, "row": row}, device_id_type=pl.DeviceIdType.MESH)


local = pltpu.make_async_copy


def place():
    col, row = lax.axis_index("col"), lax.axis_index("row")
    return col, row, col // XS, col % XS, row // 2, row % 2


def slots_of(fill, base, first, slots, halves):
    where = [jnp.int32(0)] * slots
    seen = jnp.int32(0)
    for n in range(halves):
        on = fill[n % 2, base + n // 2] != 0
        for k in range(slots):
            hit = jnp.logical_and(on, seen == first + k)
            where[k] = jnp.where(hit, n, where[k])
        seen = seen + jnp.where(on, 1, 0)
    return where


class SlabGather:
    def __init__(self, staged, queued, packed, slab, q_send, q_recv, x_send, x_recv, x_own, r_send, r_recv):
        self.refs = staged, queued, packed, slab
        self.q_send, self.q_recv, self.x_own = q_send, q_recv, x_own
        self.x_send, self.x_recv, self.r_send, self.r_recv = x_send, x_recv, r_send, r_recv
        self.slots = packed.shape[0]
        self.per = staged.shape[0]

    def stage(self, panel):
        staged = self.refs[0]
        for t in range(self.per):
            for h in range(2):
                staged[t, h] = panel[8 * t : 8 * t + 8, B * h : B * h + B]

    def target(self, t):
        index = self.per * place()[0] + t
        return index // COLS, (index % ZS) * XS + (index % COLS) // ZS

    def spread(self):
        staged, queued, _, _ = self.refs
        col, row, *_ = place()

        def send(t, _):
            block, target = self.target(t)
            there = queued.at[pl.ds(2 * block, 2)]

            @pl.when(target != col)
            def _():
                remote(staged.at[t], there, self.q_send, self.q_recv, target, row).start()

            @pl.when(target == col)
            def _():
                local(staged.at[t], there, self.q_recv).start()
            return 0

        lax.fori_loop(0, self.per, send, 0)

    def along_x(self, dx):
        _, _, packed, slab = self.refs
        col, row, zi, xi, *_ = place()
        half = self.slots // 2
        return remote(packed.at[pl.ds(0, half)], slab.at[pl.ds(0, half), zi, xi],
                      self.x_send.at[dx - 1], self.x_recv.at[dx - 1], zi * XS + (xi + dx) % XS, row)

    def across_x(self, z, start, count, dx):
        slab = self.refs[3]
        col, row, zi, xi, *_ = place()
        part = slab.at[pl.ds(start, count), z, xi]
        return remote(part, part, self.x_send.at[dx + 2], self.x_recv.at[dx + 2],
                      zi * XS + (xi + dx) % XS, row)

    def pass_across(self, z):
        half = self.slots // 2
        for dx in range(1, XS):
            self.across_x(z, half, half, dx).start()

    def own(self):
        _, _, packed, slab = self.refs
        _, _, zi, xi, *_ = place()
        return local(packed, slab.at[:, zi, xi], self.x_own)

    def pack(self, where):
        _, queued, packed, _ = self.refs
        zi = place()[2]
        local(queued, queued, self.q_recv).wait()
        for k in range(self.slots):
            packed[k] = queued[where[k]]
        self.own().start()
        for dx in range(1, XS):
            self.along_x(dx).start()
        self.own().wait()
        for side in range(2):
            self.ring(1, 0, side).start()
        self.pass_across(zi)

    def source(self, step, side):
        sign = 1 if side == 0 else -1
        return (place()[2] - sign * step + ZS) % ZS

    def ring(self, kind, step, side):
        slab = self.refs[3]
        col, row, zi, xi, *_ = place()
        sign = 1 if side == 0 else -1
        half = self.slots // 2
        rows = pl.ds(kind * half, half) if step < 3 else pl.ds(kind * half + side * (half // 2), half // 2)
        part = slab.at[rows, self.source(step, side)] if kind == 0 else slab.at[rows, self.source(step, side), xi]
        target = ((zi + sign + ZS) % ZS) * XS + xi
        return remote(part, part, self.r_send.at[kind, side, step], self.r_recv.at[kind, side, step], target, row)

    def first(self):
        for dx in range(1, XS):
            self.along_x(dx).wait_recv()
        for side in range(2):
            self.ring(0, 0, side).start()
        self.next_across(1)

    def next_across(self, step):
        for side in range(2):
            self.ring(1, step - 1, side).wait_recv()
            if step < 4:
                self.ring(1, step, side).start()
        if step < 4:
            for side in range(2):
                self.pass_across(self.source(step, side))
        else:
            self.pass_across(self.source(4, 0))

    def next(self, step):
        for side in range(2):
            self.ring(0, step - 1, side).wait_recv()
            self.ring(0, step, side).start()
        self.next_across(step + 1)

    def last(self):
        staged, _, _, slab = self.refs
        half = self.slots // 2
        col = place()[0]
        for side in range(2):
            self.ring(0, 3, side).wait_recv()
        line = slab.at[pl.ds(half, half), :, 0]
        for dx in range(1, XS):
            local(line, line, self.x_recv.at[dx + 2]).wait()
            local(line, line, self.x_send.at[dx + 2]).wait()
            self.along_x(dx).wait_send()
        for kind in range(2):
            for side in range(2):
                for step in range(4):
                    self.ring(kind, step, side).wait_send()

        def sent(t, _):
            @pl.when(self.target(t)[1] != col)
            def _():
                local(staged.at[0], staged.at[0], self.q_send).wait()
            return 0

        lax.fori_loop(0, self.per, sent, 0)


def slab_scratch(per, slots):
    dma = pltpu.SemaphoreType.DMA
    return [
        pltpu.VMEM((per, 2, 8, B), F32), pltpu.VMEM((2 * per, 8, B), F32), pltpu.VMEM((slots, 8, B), F32),
        dma, dma, dma((6,)), dma((6,)), dma, dma((2, 2, 4)), dma((2, 2, 4)),
    ]


def gather_kernel(fill_any, pivot_any, panel_any, trailing, z_out, t_hi, t_lo, slab, held, fill, pivot, panel, work, full, mc,
                  in_sem, held_sem, zs_send, zs_recv, zx_send, zx_recv, ex_send, ex_recv, c_send, c_recv,
                  y_send, y_recv, k_send, k_recv, staged, queued, packed, *slab_sems):
    col, row, zi, xi, y, core = place()
    halves = queued.shape[0]
    per = staged.shape[0]
    blocks = halves // 2
    gather = SlabGather(staged, queued, packed, slab, *slab_sems)
    loads = [
        local(fill_any, fill, in_sem.at[0]),
        local(pivot_any, pivot, in_sem.at[1]),
        local(panel_any, panel, in_sem.at[2]),
    ]
    for load in loads:
        load.start()

    def column_target(t):
        index = per * col + t
        target_col, target_row = 6 * row + index // 64, index % 8
        own = jnp.logical_and(target_col == col, target_row == row)
        return (index % 64) // 8, target_col, target_row, own

    def column_sends(t):
        _, target_col, _, own = column_target(t)
        return jnp.logical_and(target_col < COLS, jnp.logical_not(own))

    barrier = pltpu.get_barrier_semaphore()

    def greet(c, r):
        pl.semaphore_signal(barrier, inc=1, device_id={"col": c, "row": r}, device_id_type=pl.DeviceIdType.MESH)

    def greet_slab(i, _):
        greet((col + i) % COLS, row)
        return 0

    lax.fori_loop(1, COLS, greet_slab, 0)
    greet(col, 2 * y + 1 - core)
    for dy in range(1, 4):
        greet(col, 2 * ((y + dy) % 4) + core)

    def greet_column(s, _):
        source = (64 * (col % 6) + 8 * s + row) // per
        source_row = col // 6

        @pl.when(jnp.logical_not(jnp.logical_and(source == col, source_row == row)))
        def _():
            greet(source, source_row)
        return 0

    lax.fori_loop(0, 8, greet_column, 0)
    expected = jnp.int32(COLS - 1 + 4)
    for t in range(per):
        expected = expected + jnp.where(column_sends(t), 1, 0)
    z_out[...] = jnp.zeros_like(z_out)
    for load in loads:
        load.wait()
    gather.stage(panel)
    pl.semaphore_wait(barrier, expected)

    def pivot_z(dz):
        target = ((zi + dz) % ZS) * XS + xi
        return remote(pivot.at[core], full.at[zi, xi, core], zs_send, zs_recv.at[zi], target, row)

    def pivot_from(z):
        part = full.at[z, xi, core]
        return local(part, part, zs_recv.at[z])

    def pivot_x(part, dx):
        rows = full.at[pl.ds(0, 2), xi, core] if part == 0 else full.at[pl.ds(2, ZS - 2), xi, core]
        return remote(rows, rows, zx_send.at[part, dx - 1], zx_recv.at[part, dx - 1],
                      zi * XS + (xi + dx) % XS, row)

    def exchange(part):
        rows = full.at[pl.ds(0, 2), :, core] if part == 0 else full.at[pl.ds(2, ZS - 2), :, core]
        return remote(rows, rows, ex_send.at[part], ex_recv.at[part], col, 2 * y + 1 - core)

    local(pivot.at[core], full.at[zi, xi, core], zs_recv.at[zi]).start()
    for dz in (4, 3, 5, 2, 6, 1, 7):
        pivot_z(dz).start()
    gather.spread()

    def send_column(t, _):
        slot, target_col, target_row, own = column_target(t)
        there = mc.at[slot, target_row]

        @pl.when(column_sends(t))
        def _():
            remote(staged.at[t], there, c_send, c_recv, target_col, target_row).start()

        @pl.when(own)
        def _():
            local(staged.at[t], there, c_recv).start()
        return 0

    lax.fori_loop(0, per, send_column, 0)
    where = slots_of(fill, blocks * row, 0, SLOTS, halves)
    for z in range(2):
        pivot_from(z).wait()
    for dx in range(1, XS):
        pivot_x(0, dx).start()
    for z in range(2, ZS):
        pivot_from(z).wait()
    for dx in range(1, XS):
        pivot_x(1, dx).start()
    gather.pack(where)
    for dx in range(1, XS):
        pivot_x(0, dx).wait_recv()
    exchange(0).start()
    hold = local(trailing, held, held_sem)
    hold.start()

    def pivot_rest():
        for dx in range(1, XS):
            pivot_x(1, dx).wait_recv()
        exchange(1).start()

    def column_y(dy):
        part = mc.at[:, row]
        return remote(part, part, y_send.at[dy - 1], y_recv.at[dy - 1], col, 2 * ((y + dy) % 4) + core)

    def column_first():
        part = mc.at[:, row]
        local(part, part, c_recv).wait()
        for dy in range(1, 4):
            column_y(dy).start()

    def column_core(i):
        part = mc.at[:, 2 * i + core]
        return remote(part, part, k_send.at[i], k_recv.at[i], col, 2 * y + 1 - core)

    def column_next():
        for dy in range(1, 4):
            column_y(dy).wait_recv()
        for i in range(4):
            column_core(i).start()

    plan = {
        (0, 3): pivot_rest,
        (0, 4): gather.first,
        (0, 11): column_first,
        (1, 2): functools.partial(gather.next, 1),
        (1, 15): functools.partial(gather.next, 2),
        (2, 6): column_next,
        (2, 14): functools.partial(gather.next, 3),
    }

    n = z_out.shape[0]
    exchange(0).wait_recv()
    for k in range(n // TILE):
        lo, hi = k * TILE, (k + 1) * TILE
        if k == 0:
            groups = [full[g // 8, (g // 2) % 4, g % 2, :, lo:hi] for g in range(TILE // 8)]
        else:
            groups = [work[lo + 8 * g : lo + 8 * g + 8, lo:hi] for g in range(TILE // 8)]

        def hook(g, k=k):
            if (k, g) in plan:
                plan[k, g]()

        rows = invert_tile(groups, hook)
        for g in range(TILE // 8):
            z_out[lo + 8 * g : lo + 8 * g + 8, lo:hi] = rows[g]
        zk = z_out[lo:hi, lo:hi]
        if k > 0:
            z_out[lo:hi, :lo] = mm(zk, z_out[lo:hi, :lo], NN)
        if hi < n:
            if k == 0:
                exchange(1).wait_recv()
                below = full[2:].reshape(n - hi, n)
            else:
                below = work[hi:, :]
            p = mm(below[:, lo:hi], zk, NT)
            work[hi:, hi:] = below[:, hi:] - mm(p, p, NT)
            z_out[hi:, :hi] = z_out[hi:, :hi] - mm(p, z_out[lo:hi, :hi], NN)

    for i in range(4):
        column_core(i).wait_recv()

    def flag(block, h):
        return jnp.where(fill[h, block] != 0, 1.0, 0.0).astype(F32)

    rows = []
    for i in range(2):
        part = mc[4 * i : 4 * i + 4]
        rows.append(jnp.concatenate(
            [part[:, :, h].reshape(B, B) * flag(2 * col + i, h) for h in range(2)], axis=1))
    zs = split(z_out[...])
    xc = mm3(zs, split(jnp.concatenate(rows, axis=0)), NT)
    t_hi[...], t_lo[...] = split(mm3(zs, split(xc), TN))

    gather.last()
    hold.wait()
    for i in range(4):
        column_core(i).wait_send()
    for dy in range(1, 4):
        column_y(dy).wait_send()
    for part in range(2):
        exchange(part).wait_send()
        for dx in range(1, XS):
            pivot_x(part, dx).wait_send()
    local(full.at[pl.ds(0, ZS - 1), 0, core], full.at[pl.ds(0, ZS - 1), 0, core], zs_send).wait()

    def sent_column(t, _):
        @pl.when(column_sends(t))
        def _():
            local(staged.at[0], staged.at[0], c_send).wait()
        return 0

    lax.fori_loop(0, per, sent_column, 0)


def gather_and_factor(fill, pivot, panel, trailing):
    n = panel.shape[1]
    per = panel.shape[0] // 8
    dma = pltpu.SemaphoreType.DMA
    vmem = pl.BlockSpec(memory_space=pltpu.VMEM)
    anywhere = pl.BlockSpec(memory_space=pl.ANY)
    return pl.pallas_call(
        gather_kernel,
        out_shape=(
            jax.ShapeDtypeStruct((n, n), F32),
            jax.ShapeDtypeStruct((n, n), BF16),
            jax.ShapeDtypeStruct((n, n), BF16),
            jax.ShapeDtypeStruct((SLOTS, ZS, XS, 8, B), F32),
            jax.ShapeDtypeStruct(trailing.shape, F32),
        ),
        in_specs=[pl.BlockSpec(memory_space=pltpu.HBM)] * 4,
        out_specs=(vmem, vmem, vmem, anywhere, vmem),
        scratch_shapes=[
            pltpu.SMEM(fill.shape, jnp.int32),
            pltpu.VMEM((2, 8, n), F32),
            pltpu.VMEM(panel.shape, F32),
            pltpu.VMEM((n, n), F32),
            pltpu.VMEM((ZS, XS, 2, 8, n), F32),
            pltpu.VMEM((8, ROWS, 2, 8, B), F32),
            dma((3,)), dma, dma, dma((ZS,)), dma((2, 3)), dma((2, 3)), dma((2,)), dma((2,)), dma, dma,
            dma((3,)), dma((3,)), dma((4,)), dma((4,)),
        ] + slab_scratch(per, SLOTS),
        compiler_params=pltpu.CompilerParams(
            has_side_effects=True, collective_id=0, vmem_limit_bytes=30 << 20),
        name="gather_and_factor",
    )(fill, pivot.reshape(2, 8, n), panel, trailing)


def gather_more_kernel(first, fill, panel, slab, staged, queued, packed, *sems):
    row = lax.axis_index("row")
    halves = queued.shape[0]
    gather = SlabGather(staged, queued, packed, slab, *sems)
    gather.stage(panel)
    gather.spread()
    gather.pack(slots_of(fill, halves // 2 * row, first[0], SLOTS, halves))
    gather.first()
    for step in range(1, 4):
        gather.next(step)
    gather.last()


def gather_more(first, fill, panel):
    per = panel.shape[0] // 8
    smem = pl.BlockSpec(memory_space=pltpu.SMEM)
    return pl.pallas_call(
        gather_more_kernel,
        out_shape=jax.ShapeDtypeStruct((SLOTS, ZS, XS, 8, B), F32),
        in_specs=[smem, smem, pl.BlockSpec(memory_space=pltpu.VMEM)],
        out_specs=pl.BlockSpec(memory_space=pl.ANY),
        scratch_shapes=slab_scratch(per, SLOTS),
        compiler_params=pltpu.CompilerParams(has_side_effects=True, vmem_limit_bytes=60 << 20),
        name="gather_more",
    )(first, fill, panel)


def add_blocks(fill, base, first, t_hi, t_lo, slab, blocks, before, after):
    seen = jnp.int32(0)
    for b in range(blocks.shape[0]):
        before(b)
        for h in range(2):
            on = fill[h, base + b] != 0
            slot = seen - first

            @pl.when(jnp.logical_and(on, jnp.logical_and(slot >= 0, slot < SLOTS)))
            def _(b=b, h=h, slot=slot):
                m = split(jnp.concatenate([slab[slot, :, x].reshape(8 * ZS, B) for x in range(XS)], axis=0))
                t = (t_hi[B * h : B * h + B], t_lo[B * h : B * h + B])
                blocks[b] = blocks[b] - mm3(m, t, NN)

            seen = seen + jnp.where(on, 1, 0)
        after(b)


def update_kernel(fill_any, z, t_hi, t_lo, slab, panel, held, updated, own, most,
                  fill, blocks, in_sem, write_sem):
    col, row = lax.axis_index("col"), lax.axis_index("row")
    count = blocks.shape[0]
    base = count * row
    get_fill = local(fill_any, fill, in_sem)
    get_fill.start()
    get_fill.wait()

    def touched(b):
        return jnp.logical_or(fill[0, base + b] != 0, fill[1, base + b] != 0)

    def write(b):
        return local(blocks.at[b], updated.at[pl.ds(B * b, B)], write_sem.at[b])

    def keep(b):
        return local(held.at[pl.ds(B * b, B)], updated.at[pl.ds(B * b, B)], write_sem.at[b])

    for b in range(count):
        @pl.when(jnp.logical_not(touched(b)))
        def _(b=b):
            keep(b).start()

    top = jnp.int32(0)
    for r in range(ROWS):
        total = jnp.int32(0)
        for b in range(count):
            for h in range(2):
                total = total + jnp.where(fill[h, count * r + b] != 0, 1, 0)
        top = jnp.maximum(top, total)
    most[0] = top

    masked = []
    for t in range(panel.shape[0] // 8):
        block = base + (panel.shape[0] * col + 8 * t) // B
        masked.append(jnp.concatenate(
            [panel[8 * t : 8 * t + 8, B * h : B * h + B]
             * jnp.where(fill[h, block] != 0, 1.0, 0.0).astype(F32) for h in range(2)], axis=1))
    own[...] = mm(jnp.concatenate(masked, axis=0), z[...], NT)

    def before(b):
        @pl.when(touched(b))
        def _():
            blocks[b] = held[B * b : B * b + B]

    def after(b):
        @pl.when(touched(b))
        def _():
            write(b).start()

    add_blocks(fill, base, 0, t_hi, t_lo, slab, blocks, before, after)
    for b in range(count):
        write(b).wait()


def apply_update(fill, z, t_hi, t_lo, slab, panel, held):
    count = held.shape[0] // B
    width = held.shape[1]
    dma = pltpu.SemaphoreType.DMA
    vmem = pl.BlockSpec(memory_space=pltpu.VMEM)
    hbm = pl.BlockSpec(memory_space=pltpu.HBM)
    smem = pl.BlockSpec(memory_space=pltpu.SMEM)
    return pl.pallas_call(
        update_kernel,
        out_shape=(
            jax.ShapeDtypeStruct(held.shape, F32),
            jax.ShapeDtypeStruct(panel.shape, F32),
            jax.ShapeDtypeStruct((1,), jnp.int32),
        ),
        in_specs=[hbm, vmem, vmem, vmem, vmem, vmem, vmem],
        out_specs=(hbm, vmem, smem),
        scratch_shapes=[
            pltpu.SMEM(fill.shape, jnp.int32),
            pltpu.VMEM((count, B, width), F32),
            dma, dma((count,)),
        ],
        compiler_params=pltpu.CompilerParams(vmem_limit_bytes=30 << 20),
        name="apply_update",
    )(fill, z, t_hi, t_lo, slab, panel, held)


def update_more_kernel(first, fill, t_hi, t_lo, slab, before_any, after_any, blocks, read_sem, write_sem):
    count = blocks.shape[0]
    base = count * lax.axis_index("row")

    def read(b):
        return local(before_any.at[pl.ds(B * b, B)], blocks.at[b], read_sem.at[b])

    def write(b):
        return local(blocks.at[b], after_any.at[pl.ds(B * b, B)], write_sem.at[b])

    for b in range(count):
        read(b).start()
    add_blocks(fill, base, first[0], t_hi, t_lo, slab, blocks,
               lambda b: read(b).wait(), lambda b: write(b).start())
    for b in range(count):
        write(b).wait()


def update_more(first, fill, t_hi, t_lo, slab, updated):
    count = updated.shape[0] // B
    dma = pltpu.SemaphoreType.DMA
    vmem = pl.BlockSpec(memory_space=pltpu.VMEM)
    hbm = pl.BlockSpec(memory_space=pltpu.HBM)
    smem = pl.BlockSpec(memory_space=pltpu.SMEM)
    return pl.pallas_call(
        update_more_kernel,
        out_shape=jax.ShapeDtypeStruct(updated.shape, F32),
        in_specs=[smem, smem, vmem, vmem, vmem, hbm],
        out_specs=hbm,
        scratch_shapes=[
            pltpu.VMEM((count, B, updated.shape[1]), F32), dma((count,)), dma((count,))],
        input_output_aliases={5: 0},
        compiler_params=pltpu.CompilerParams(vmem_limit_bytes=60 << 20),
        name="update_more",
    )(first, fill, t_hi, t_lo, slab, updated)


def per_device(trailing, panel_rows, pivot_block, panel_fill):
    fill = panel_fill.T
    z, t_hi, t_lo, slab, held = gather_and_factor(fill, pivot_block, panel_rows, trailing)
    updated, own, most = apply_update(fill, z, t_hi, t_lo, slab, panel_rows, held)

    def body(state):
        first, updated = state
        more = gather_more(first, fill, panel_rows)
        return first + SLOTS, update_more(first, fill, t_hi, t_lo, more, updated)

    start = jnp.full((1,), SLOTS, jnp.int32)
    _, updated = lax.while_loop(lambda state: state[0][0] < most[0], body, (start, updated))
    return updated, own


def solution(mesh):
    in_specs = (P("row", "col"), P(("row", "col"), None), P("col", None), P())
    out_specs = (P("row", "col"), P(("row", "col"), None))
    return jax.shard_map(
        per_device, mesh=mesh, in_specs=in_specs, out_specs=out_specs, check_vma=False
    )
```

time: 403 us -> 125 us (0.31)
  waiting for transfers between devices: 232 us -> 0 us
  other arithmetic: 124 us -> 0 us
  Pallas kernels: 0 us -> 117 us
  matrix products: 19.6 us -> 0 us
  between operations: 16.6 us -> 0.84 us
  local copies, waits for them, and re-layouts: 10.3 us -> 3.55 us
    all_gather x2 -> x0, waiting for transfers between devices: 164 us -> none  [the longest x1 85.5 us: per_device(): row_side = lax.all_gather(own_factor, 'col', axis=0, tiled=True)]
    another operation x18 -> x0, other arithmetic: 119 us -> none  [the longest x14 78.7 us: per_device(): factor = jnp.linalg.cholesky(pivot_full)]
    pallas_call x0 -> x4, Pallas kernels: none -> 117 us  [the longest x1 60.3 us: gather_and_factor(): pl.pallas_call(gather_kernel, out_shape=(jax.ShapeDtypeStruct((n, n), F32...]
    psum x1 -> x0, waiting for transfers between devices: 67.1 us -> none  [from_root(): return lax.psum(kept, axis)]
    dot_general x2 -> x0, matrix products: 16 us -> none  [the longest x1 15.1 us: per_device(): lax.dot_general(row_side, column_side, (((1,), (1,)), ((), ())), precisio...]
    another operation x17 -> x0, local copies, waits for them, and re-layouts: 8.54 us -> none
  transfers between devices with their start and end apart: 3 -> 0, of which waited for: 3 -> 0; matrix products, arithmetic and copies ran while one was open for 1% -> 0% of each run, Pallas kernels for 0% -> 0%
where the time goes in v1:
time: 125 us; the launch traced here: 123 us
  Pallas kernels  117 us (94%)
  local copies, waits for them, and re-layouts  3.55 us (3%)
  loops' own time  1.39 us (1%)
    pallas_call x1, Pallas kernels, gather_and_factor(): pl.pallas_call(gather_kernel, out_shape=(jax.ShapeDtypeStruct((n, n), F32...  60.3 us
    pallas_call x1, Pallas kernels, gather_more(): pl.pallas_call(gather_more_kernel, out_shape=jax.ShapeDtypeStruct((SLOTS,...  44.9 us
    pallas_call x1, Pallas kernels, update_more(): pl.pallas_call(update_more_kernel, out_shape=jax.ShapeDtypeStruct(updated...  7.07 us
    pallas_call x1, Pallas kernels, apply_update(): pl.pallas_call(update_kernel, out_shape=(jax.ShapeDtypeStruct(held.shape,...  4.83 us
    unnamed x8, local copies, waits for them, and re-layouts  3.55 us

profile of v1, /device:TPU:6, one launch (start us, length us, event | category | flops | bytes accessed | tf_op | source)
XLA Modules:
  0.0 122.9 jit_solution(5872285659205662094)
XLA Ops:
  0.6 0.0 copy-start.3
  0.6 0.0 copy-start
  0.7 2.8 %copy-done = f32[3072,512]{1,0:T(8,128)S(1)} copy-done((f32[3072,512]{1,0:T(8,128)S(1)}, f32[3072,512]{1,0:T(8,128)}, u32[]{:S(2)}) %copy-start) | copy-done | bytes 6291480
  3.4 0.0 copy-start.1
  3.4 0.8 copy-done.1
  4.2 0.0 copy-start.2
  4.2 60.3 %gather_and_factor.1 = (f32[512,512]{1,0:T(8,128)S(1)}, bf16[512,512]{1,0:T(8,128)(2,1)S(1)}, bf16[512,512]{1,0:T(8,128)(2,1)S(1)}, f32[8,8,4,8,256]{4,3,2,1,0:T(8,128)S(1)}, f32[3072,512]{1,0:T(8,128)S(1)}) custom-call(s32[2,96]{1,0:T(2,128)} %bitcast.5, f32[2,8,512]{2,1,0:T(8,128)S(1)} %bitcast.4, f32[96,512]{1,0:T(8,128)} %panel.1, f32[3072,512]{1,0:T(8,128)S(1)} %copy-done), custom_call_target="tpu_custom_call" | custom-call | tf_op jit(solution)/shard_map/gather_and_factor/pallas_call | solution.py:492
  64.5 0.0 copy-done.3
  64.5 0.0 copy-done.2
  64.5 4.8 %apply_update.1 = (f32[3072,512]{1,0:T(8,128)}, f32[96,512]{1,0:T(8,128)}, s32[1]{0:T(128)}) custom-call(s32[2,96]{1,0:T(2,128)S(1)} %bitcast.6, f32[512,512]{1,0:T(8,128)S(1)} %get-tuple-element.48.z, bf16[512,512]{1,0:T(8,128)(2,1)S(1)} %get-tuple-element.113.t_hi, bf16[512,512]{1,0:T(8,128)(2,1)S(1)} %get-tuple-element.114.t_lo, ...), custom_call_target="tpu_custom_call" | custom-call | tf_op jit(solution)/shard_map/apply_update/pallas_call | solution.py:626
  69.3 53.4 %while.10 = (s32[1]{0:T(128)}, f32[3072,512]{1,0:T(8,128)}, s32[1]{0:T(128)}, s32[2,96]{1,0:T(2,128)S(1)}, f32[96,512]{1,0:T(8,128)S(1)}, /*index=5*/bf16[512,51...) while((s32[1]{0:T(128)}, f32[3072,512]{1,0:T(8,128)}, s32[1]{0:T(128)}, s32[2,96]{1,0:T(2,128)S(1)}, ...), condition=%wide.region_1.0_spmd, body=%wide.region_0.0_spmd | while | flops 2 | bytes 85 | solution.py:693
  70.0 44.9 %gather_more.1.slab = f32[8,8,4,8,256]{4,3,2,1,0:T(8,128)} custom-call(s32[1]{0:T(128)} %get-tuple-element.116.first, s32[2,96]{1,0:T(2,128)S(1)} %get-tuple-element.127.fill, f32[96,512]{1,0:T(8,128)S(1)} %get-tuple-element.128.panel), custom_call_target="tpu_custom_call" | custom-call | tf_op jit(solution)/shard_map/while/body/gather_more/pallas_call | solution.py:535
  115.0 7.1 %update_more.1 = f32[3072,512]{1,0:T(8,128)} custom-call(s32[1]{0:T(128)} %get-tuple-element.116.first, s32[2,96]{1,0:T(2,128)S(1)} %get-tuple-element.127.fill, bf16[512,512]{1,0:T(8,128)(2,1)S(1)} %get-tuple-element.129.t_hi, bf16[512,512]{1,0:T(8,128)(2,1)S(1)} %get-tuple-element.130.t_lo, ...), custom_call_target="tpu_custom_call", output_to_operand_aliasing={{}: (5, {})} | custom-call | tf_op jit(solution)/shard_map/while/body/update_more/pallas_call | solution.py:669
Async XLA Ops:
  0.6 63.9 %copy-start.3 = (s32[96,2]{0,1:T(2,128)S(1)}, s32[96,2]{0,1:T(2,128)}, u32[]{:S(2)}) copy-start(s32[96,2]{0,1:T(2,128)} %param.9) | copy-start | bytes 2308
  0.6 2.8 %copy-start = (f32[3072,512]{1,0:T(8,128)S(1)}, f32[3072,512]{1,0:T(8,128)}, u32[]{:S(2)}) copy-start(f32[3072,512]{1,0:T(8,128)} %trailing.1) | copy-start | bytes 18874372
  3.4 0.8 copy-start.1
  4.2 60.3 %copy-start.2 = (f32[96,512]{1,0:T(8,128)S(1)}, f32[96,512]{1,0:T(8,128)}, u32[]{:S(2)}) copy-start(f32[96,512]{1,0:T(8,128)} %panel.1) | copy-start | bytes 589828

commit v2 on v1

--- a/solution.py
+++ b/solution.py
@@ -272,8 +272,8 @@
     ]
 
 
-def gather_kernel(fill_any, pivot_any, panel_any, trailing, z_out, t_hi, t_lo, slab, held, fill, pivot, panel, work, full, mc,
-                  in_sem, held_sem, zs_send, zs_recv, zx_send, zx_recv, ex_send, ex_recv, c_send, c_recv,
+def gather_kernel(fill_any, pivot_any, panel_any, z_out, t_hi, t_lo, slab, fill, pivot, panel, work, full, mc,
+                  in_sem, zs_send, zs_recv, zx_send, zx_recv, ex_send, ex_recv, c_send, c_recv,
                   y_send, y_recv, k_send, k_recv, staged, queued, packed, *slab_sems):
     col, row, zi, xi, y, core = place()
     halves = queued.shape[0]
@@ -380,9 +380,6 @@
     for dx in range(1, XS):
         pivot_x(0, dx).wait_recv()
     exchange(0).start()
-    hold = local(trailing, held, held_sem)
-    hold.start()
-
     def pivot_rest():
         for dx in range(1, XS):
             pivot_x(1, dx).wait_recv()
@@ -463,7 +460,6 @@
     t_hi[...], t_lo[...] = split(mm3(zs, split(xc), TN))
 
     gather.last()
-    hold.wait()
     for i in range(4):
         column_core(i).wait_send()
     for dy in range(1, 4):
@@ -483,7 +479,7 @@
     lax.fori_loop(0, per, sent_column, 0)
 
 
-def gather_and_factor(fill, pivot, panel, trailing):
+def gather_and_factor(fill, pivot, panel):
     n = panel.shape[1]
     per = panel.shape[0] // 8
     dma = pltpu.SemaphoreType.DMA
@@ -496,10 +492,9 @@
             jax.ShapeDtypeStruct((n, n), BF16),
             jax.ShapeDtypeStruct((n, n), BF16),
             jax.ShapeDtypeStruct((SLOTS, ZS, XS, 8, B), F32),
-            jax.ShapeDtypeStruct(trailing.shape, F32),
         ),
-        in_specs=[pl.BlockSpec(memory_space=pltpu.HBM)] * 4,
-        out_specs=(vmem, vmem, vmem, anywhere, vmem),
+        in_specs=[pl.BlockSpec(memory_space=pltpu.HBM)] * 3,
+        out_specs=(vmem, vmem, vmem, anywhere),
         scratch_shapes=[
             pltpu.SMEM(fill.shape, jnp.int32),
             pltpu.VMEM((2, 8, n), F32),
@@ -507,13 +502,14 @@
             pltpu.VMEM((n, n), F32),
             pltpu.VMEM((ZS, XS, 2, 8, n), F32),
             pltpu.VMEM((8, ROWS, 2, 8, B), F32),
-            dma((3,)), dma, dma, dma((ZS,)), dma((2, 3)), dma((2, 3)), dma((2,)), dma((2,)), dma, dma,
+            dma((3,)), dma, dma((ZS,)), dma((2, 3)), dma((2, 3)), dma((2,)), dma((2,)), dma, dma,
             dma((3,)), dma((3,)), dma((4,)), dma((4,)),
         ] + slab_scratch(per, SLOTS),
         compiler_params=pltpu.CompilerParams(
             has_side_effects=True, collective_id=0, vmem_limit_bytes=30 << 20),
+        cost_estimate=pl.CostEstimate(flops=40_000_000_000, bytes_accessed=60_000_000, transcendentals=0),
         name="gather_and_factor",
-    )(fill, pivot.reshape(2, 8, n), panel, trailing)
+    )(fill, pivot.reshape(2, 8, n), panel)
 
 
 def gather_more_kernel(first, fill, panel, slab, staged, queued, packed, *sems):
@@ -681,8 +677,8 @@
 
 def per_device(trailing, panel_rows, pivot_block, panel_fill):
     fill = panel_fill.T
-    z, t_hi, t_lo, slab, held = gather_and_factor(fill, pivot_block, panel_rows, trailing)
-    updated, own, most = apply_update(fill, z, t_hi, t_lo, slab, panel_rows, held)
+    z, t_hi, t_lo, slab = gather_and_factor(fill, pivot_block, panel_rows)
+    updated, own, most = apply_update(fill, z, t_hi, t_lo, slab, panel_rows, trailing)
 
     def body(state):
         first, updated = state

time: 125 us -> 69 us (0.55)
  the two profiles are of different devices: /device:TPU:6 before, /device:TPU:1 now
where the time goes in v2:
time: 69 us; the launch traced here: 68.9 us
  Pallas kernels  66.6 us (97%)
  between operations  0.84 us (1%)
  local copies, waits for them, and re-layouts  0.76 us (1%)
    pallas_call x1, Pallas kernels, gather_and_factor(): pl.pallas_call(gather_kernel, out_shape=(jax.ShapeDtypeStruct((n, n), F32...  60.5 us
    pallas_call x1, Pallas kernels, apply_update(): pl.pallas_call(update_kernel, out_shape=(jax.ShapeDtypeStruct(held.shape,...  6.1 us

profile of v2, /device:TPU:1, one launch (start us, length us, event | category | flops | bytes accessed | tf_op | source)
XLA Modules:
  0.0 68.9 jit_solution(9926217050019139607)
XLA Ops:
  0.6 0.0 copy-start.1
  0.6 0.7 %copy-done.1 = f32[16,512]{1,0:T(8,128)S(1)} copy-done((f32[16,512]{1,0:T(8,128)S(1)}, f32[16,512]{1,0:T(8,128)}, u32[]{:S(2)}) %copy-start.1) | copy-done | bytes 32792
  1.4 0.0 copy-start
  1.4 0.0 copy-start.2
  1.4 0.0 copy-start.3
  1.4 60.5 %gather_and_factor.1 = (f32[512,512]{1,0:T(8,128)S(1)}, bf16[512,512]{1,0:T(8,128)(2,1)S(1)}, bf16[512,512]{1,0:T(8,128)(2,1)S(1)}, f32[8,8,4,8,256]{4,3,2,1,0:T(8,128)S(1)}) custom-call(s32[2,96]{1,0:T(2,128)} %bitcast.5, f32[2,8,512]{2,1,0:T(8,128)S(1)} %bitcast.4, f32[96,512]{1,0:T(8,128)} %panel.1), custom_call_target="tpu_custom_call" | custom-call | flops 40000000000 | bytes 60000000 | tf_op jit(solution)/shard_map/gather_and_factor/pallas_call | solution.py:488
  61.9 0.0 copy-done
  61.9 0.0 copy-done.2
  61.9 0.0 copy-done.3
  61.9 6.1 %apply_update.1 = (f32[3072,512]{1,0:T(8,128)}, f32[96,512]{1,0:T(8,128)}, s32[1]{0:T(128)}) custom-call(s32[2,96]{1,0:T(2,128)S(1)} %bitcast.6, f32[512,512]{1,0:T(8,128)S(1)} %get-tuple-element.47.z, bf16[512,512]{1,0:T(8,128)(2,1)S(1)} %get-tuple-element.111.t_hi, bf16[512,512]{1,0:T(8,128)(2,1)S(1)} %get-tuple-element.112.t_lo, ...), custom_call_target="tpu_custom_call" | custom-call | tf_op jit(solution)/shard_map/apply_update/pallas_call | solution.py:622
  68.0 0.7 while.10
Async XLA Ops:
  0.6 0.8 %copy-start.1 = (f32[16,512]{1,0:T(8,128)S(1)}, f32[16,512]{1,0:T(8,128)}, u32[]{:S(2)}) copy-start(f32[16,512]{1,0:T(8,128)} %param.8) | copy-start | bytes 98308
  1.4 60.5 %copy-start = (f32[3072,512]{1,0:T(8,128)S(1)}, f32[3072,512]{1,0:T(8,128)}, u32[]{:S(2)}) copy-start(f32[3072,512]{1,0:T(8,128)} %held.1) | copy-start | bytes 18874372
  1.4 60.5 %copy-start.2 = (f32[96,512]{1,0:T(8,128)S(1)}, f32[96,512]{1,0:T(8,128)}, u32[]{:S(2)}) copy-start(f32[96,512]{1,0:T(8,128)} %panel.1) | copy-start | bytes 589828
  1.4 60.5 %copy-start.3 = (s32[96,2]{0,1:T(2,128)S(1)}, s32[96,2]{0,1:T(2,128)}, u32[]{:S(2)}) copy-start(s32[96,2]{0,1:T(2,128)} %param.9) | copy-start | bytes 2308

commit v3 on v2

--- a/solution.py
+++ b/solution.py
@@ -407,12 +407,12 @@
 
     plan = {
         (0, 3): pivot_rest,
-        (0, 4): gather.first,
-        (0, 11): column_first,
-        (1, 2): functools.partial(gather.next, 1),
-        (1, 15): functools.partial(gather.next, 2),
-        (2, 6): column_next,
-        (2, 14): functools.partial(gather.next, 3),
+        (0, 8): gather.first,
+        (0, 14): column_first,
+        (1, 8): functools.partial(gather.next, 1),
+        (2, 6): functools.partial(gather.next, 2),
+        (2, 10): column_next,
+        (3, 4): functools.partial(gather.next, 3),
     }
 
     n = z_out.shape[0]

time: 69 us -> 66 us (0.957)
  the two profiles are of different devices: /device:TPU:1 before, /device:TPU:6 now
where the time goes in v3:
time: 66 us; the launch traced here: 65.5 us
  Pallas kernels  63.2 us (96%)
  between operations  0.84 us (1%)
  local copies, waits for them, and re-layouts  0.76 us (1%)
  loops' own time  0.69 us (1%)
    pallas_call x1, Pallas kernels, gather_and_factor(): pl.pallas_call(gather_kernel, out_shape=(jax.ShapeDtypeStruct((n, n), F32...  57.4 us
    pallas_call x1, Pallas kernels, apply_update(): pl.pallas_call(update_kernel, out_shape=(jax.ShapeDtypeStruct(held.shape,...  5.79 us

profile of v3, /device:TPU:6, one launch (start us, length us, event | category | flops | bytes accessed | tf_op | source)
XLA Modules:
  0.0 65.5 jit_solution(6805920174556235085)
XLA Ops:
  0.6 0.0 copy-start.1
  0.6 0.7 %copy-done.1 = f32[16,512]{1,0:T(8,128)S(1)} copy-done((f32[16,512]{1,0:T(8,128)S(1)}, f32[16,512]{1,0:T(8,128)}, u32[]{:S(2)}) %copy-start.1) | copy-done | bytes 32792
  1.4 0.0 copy-start
  1.4 0.0 copy-start.2
  1.4 0.0 copy-start.3
  1.4 57.4 %gather_and_factor.1 = (f32[512,512]{1,0:T(8,128)S(1)}, bf16[512,512]{1,0:T(8,128)(2,1)S(1)}, bf16[512,512]{1,0:T(8,128)(2,1)S(1)}, f32[8,8,4,8,256]{4,3,2,1,0:T(8,128)S(1)}) custom-call(s32[2,96]{1,0:T(2,128)} %bitcast.5, f32[2,8,512]{2,1,0:T(8,128)S(1)} %bitcast.4, f32[96,512]{1,0:T(8,128)} %panel.1), custom_call_target="tpu_custom_call" | custom-call | flops 40000000000 | bytes 60000000 | tf_op jit(solution)/shard_map/gather_and_factor/pallas_call | solution.py:488
  58.8 0.0 copy-done
  58.8 0.0 copy-done.2
  58.8 0.0 copy-done.3
  58.8 5.8 %apply_update.1 = (f32[3072,512]{1,0:T(8,128)}, f32[96,512]{1,0:T(8,128)}, s32[1]{0:T(128)}) custom-call(s32[2,96]{1,0:T(2,128)S(1)} %bitcast.6, f32[512,512]{1,0:T(8,128)S(1)} %get-tuple-element.47.z, bf16[512,512]{1,0:T(8,128)(2,1)S(1)} %get-tuple-element.111.t_hi, bf16[512,512]{1,0:T(8,128)(2,1)S(1)} %get-tuple-element.112.t_lo, ...), custom_call_target="tpu_custom_call" | custom-call | tf_op jit(solution)/shard_map/apply_update/pallas_call | solution.py:622
  64.6 0.7 %while.10 = (s32[1]{0:T(128)}, f32[3072,512]{1,0:T(8,128)}, s32[1]{0:T(128)}, s32[2,96]{1,0:T(2,128)S(1)}, f32[96,512]{1,0:T(8,128)S(1)}, /*index=5*/bf16[512,51...) while((s32[1]{0:T(128)}, f32[3072,512]{1,0:T(8,128)}, s32[1]{0:T(128)}, s32[2,96]{1,0:T(2,128)S(1)}, ...), condition=%wide.region_1.0_spmd, body=%wide.region_0.0_spmd | while | flops 2 | bytes 85 | solution.py:689
Async XLA Ops:
  0.6 0.8 %copy-start.1 = (f32[16,512]{1,0:T(8,128)S(1)}, f32[16,512]{1,0:T(8,128)}, u32[]{:S(2)}) copy-start(f32[16,512]{1,0:T(8,128)} %param.8) | copy-start | bytes 98308
  1.4 57.4 %copy-start = (f32[3072,512]{1,0:T(8,128)S(1)}, f32[3072,512]{1,0:T(8,128)}, u32[]{:S(2)}) copy-start(f32[3072,512]{1,0:T(8,128)} %held.1) | copy-start | bytes 18874372
  1.4 57.4 %copy-start.2 = (f32[96,512]{1,0:T(8,128)S(1)}, f32[96,512]{1,0:T(8,128)}, u32[]{:S(2)}) copy-start(f32[96,512]{1,0:T(8,128)} %panel.1) | copy-start | bytes 589828
  1.4 57.4 %copy-start.3 = (s32[96,2]{0,1:T(2,128)S(1)}, s32[96,2]{0,1:T(2,128)}, u32[]{:S(2)}) copy-start(s32[96,2]{0,1:T(2,128)} %param.9) | copy-start | bytes 2308

commit v4 on v3

--- a/solution.py
+++ b/solution.py
@@ -63,32 +63,34 @@
         below = {h: columns(h, g) for h in range(g + 1, count)}
         wide, inv = left[g], right[g]
         final = inv
+        raw, raw_wide, raw_inv = list(pivot), wide, inv
         for r in range(0, 8, 2):
             a, b, d = (
-                spread_row(pivot[r], r),
-                spread_row(pivot[r + 1], r),
-                spread_row(pivot[r + 1], r + 1),
+                spread_row(raw[r], r),
+                spread_row(raw[r + 1], r),
+                spread_row(raw[r + 1], r + 1),
             )
             det = a * d - b * b
             scale = 1.0 / det
             an, bn, dn = a * scale, b * scale, d * scale
             m0, m1 = pivot[r], pivot[r + 1]
-            e0, e1 = spread_row(inv, r), spread_row(inv, r + 1)
+            e0, e1 = spread_row(raw_inv, r), spread_row(raw_inv, r + 1)
             over_a = 1.0 / a
             f0 = e0 * lax.rsqrt(a)
             f1 = (e1 - (b * over_a) * e0) * lax.rsqrt(det * over_a)
             final = jnp.where(sub == r, f0, jnp.where(sub == r + 1, f1, final))
 
-            def step(w):
-                w0, w1 = spread_row(w, r), spread_row(w, r + 1)
+            def step(w, ahead):
+                w0, w1 = spread_row(ahead, r), spread_row(ahead, r + 1)
                 y0 = dn * w0 - bn * w1
                 y1 = an * w1 - bn * w0
                 rest = w - (m0 * y0 + m1 * y1)
-                return jnp.where(sub == r, y0, jnp.where(sub == r + 1, y1, rest))
+                return jnp.where(sub == r, y0, jnp.where(sub == r + 1, y1, rest)), rest
 
             for q in range(r + 2, 8):
-                pivot[q] = step(pivot[q])
-            wide, inv = step(wide), step(inv)
+                pivot[q], raw[q] = step(pivot[q], raw[q])
+            wide, raw_wide = step(wide, raw_wide)
+            inv, raw_inv = step(inv, raw_inv)
         done.append(final)
         wide_rows = [spread_row(wide, r) for r in range(8)]
         inv_rows = [spread_row(inv, r) for r in range(8)]

time: 66 us -> 66.7 us (1.011)
  Pallas kernels: 63.2 us -> 63.9 us
    pallas_call x1, Pallas kernels: 5.79 us -> 6.48 us  [apply_update(): pl.pallas_call(update_kernel, out_shape=(jax.ShapeDtypeStruct(held.shape,...]
where the time goes in v4:
time: 66.7 us; the launch traced here: 66.2 us
  Pallas kernels  63.9 us (96%)
  between operations  0.84 us (1%)
  local copies, waits for them, and re-layouts  0.76 us (1%)
  loops' own time  0.69 us (1%)
    pallas_call x1, Pallas kernels, gather_and_factor(): pl.pallas_call(gather_kernel, out_shape=(jax.ShapeDtypeStruct((n, n), F32...  57.4 us
    pallas_call x1, Pallas kernels, apply_update(): pl.pallas_call(update_kernel, out_shape=(jax.ShapeDtypeStruct(held.shape,...  6.48 us

profile of v4, /device:TPU:6, one launch (start us, length us, event | category | flops | bytes accessed | tf_op | source)
XLA Modules:
  0.0 66.2 jit_solution(7333158140103944669)
XLA Ops:
  0.6 0.0 copy-start.1
  0.6 0.7 %copy-done.1 = f32[16,512]{1,0:T(8,128)S(1)} copy-done((f32[16,512]{1,0:T(8,128)S(1)}, f32[16,512]{1,0:T(8,128)}, u32[]{:S(2)}) %copy-start.1) | copy-done | bytes 32792
  1.4 0.0 copy-start
  1.4 0.0 copy-start.2
  1.4 0.0 copy-start.3
  1.4 57.4 %gather_and_factor.1 = (f32[512,512]{1,0:T(8,128)S(1)}, bf16[512,512]{1,0:T(8,128)(2,1)S(1)}, bf16[512,512]{1,0:T(8,128)(2,1)S(1)}, f32[8,8,4,8,256]{4,3,2,1,0:T(8,128)S(1)}) custom-call(s32[2,96]{1,0:T(2,128)} %bitcast.5, f32[2,8,512]{2,1,0:T(8,128)S(1)} %bitcast.4, f32[96,512]{1,0:T(8,128)} %panel.1), custom_call_target="tpu_custom_call" | custom-call | flops 40000000000 | bytes 60000000 | tf_op jit(solution)/shard_map/gather_and_factor/pallas_call | solution.py:490
  58.8 0.0 copy-done
  58.8 0.0 copy-done.2
  58.8 0.0 copy-done.3
  58.9 6.5 %apply_update.1 = (f32[3072,512]{1,0:T(8,128)}, f32[96,512]{1,0:T(8,128)}, s32[1]{0:T(128)}) custom-call(s32[2,96]{1,0:T(2,128)S(1)} %bitcast.6, f32[512,512]{1,0:T(8,128)S(1)} %get-tuple-element.47.z, bf16[512,512]{1,0:T(8,128)(2,1)S(1)} %get-tuple-element.111.t_hi, bf16[512,512]{1,0:T(8,128)(2,1)S(1)} %get-tuple-element.112.t_lo, ...), custom_call_target="tpu_custom_call" | custom-call | tf_op jit(solution)/shard_map/apply_update/pallas_call | solution.py:624
  65.3 0.7 %while.10 = (s32[1]{0:T(128)}, f32[3072,512]{1,0:T(8,128)}, s32[1]{0:T(128)}, s32[2,96]{1,0:T(2,128)S(1)}, f32[96,512]{1,0:T(8,128)S(1)}, /*index=5*/bf16[512,51...) while((s32[1]{0:T(128)}, f32[3072,512]{1,0:T(8,128)}, s32[1]{0:T(128)}, s32[2,96]{1,0:T(2,128)S(1)}, ...), condition=%wide.region_1.0_spmd, body=%wide.region_0.0_spmd | while | flops 2 | bytes 85 | solution.py:691
Async XLA Ops:
  0.6 0.8 %copy-start.1 = (f32[16,512]{1,0:T(8,128)S(1)}, f32[16,512]{1,0:T(8,128)}, u32[]{:S(2)}) copy-start(f32[16,512]{1,0:T(8,128)} %param.8) | copy-start | bytes 98308
  1.4 57.4 %copy-start = (f32[3072,512]{1,0:T(8,128)S(1)}, f32[3072,512]{1,0:T(8,128)}, u32[]{:S(2)}) copy-start(f32[3072,512]{1,0:T(8,128)} %held.1) | copy-start | bytes 18874372
  1.4 57.4 %copy-start.2 = (f32[96,512]{1,0:T(8,128)S(1)}, f32[96,512]{1,0:T(8,128)}, u32[]{:S(2)}) copy-start(f32[96,512]{1,0:T(8,128)} %panel.1) | copy-start | bytes 589828
  1.4 57.5 %copy-start.3 = (s32[96,2]{0,1:T(2,128)S(1)}, s32[96,2]{0,1:T(2,128)}, u32[]{:S(2)}) copy-start(s32[96,2]{0,1:T(2,128)} %param.9) | copy-start | bytes 2308
